TPU v7x, 32 devices: a whole 2x2x4 slice. The times are simulated.
32 devices in a mesh: dp: 4 (over y, core), seq: 8 (over z, x).
Axes of the slice: x: 2, y: 2, z: 4, core: 2. Of those that a mesh axis runs over, the one named last changes fastest.
Arguments:
- queries: bfloat16 [32768, 1024], P(('dp', 'seq')), parts along dimension 0, may hold values from -6 to 6
- keys: bfloat16 [32768, 1024], P(('dp', 'seq')), parts along dimension 0, may hold values from -6 to 6
- values: bfloat16 [32768, 1024], P(('dp', 'seq')), parts along dimension 0, may hold values from -6 to 6
Outputs:
- attended: bfloat16 [32768, 1024], P(('dp', 'seq')), parts along dimension 0
- far_attended: bfloat16 [1024, 1024], P(('dp', 'seq')), parts along dimension 0
There are 4 independent parts, one for each index of `dp`. A program takes and returns all parts, laid end to end along the dimension named above; each array names one. Nothing has to cross between parts.
All inputs are finite; a program needn't handle non-finite values.
Results may differ from a plain program's by a relative error of at most 0.0095.
Values may be sent and summed in bfloat16 or wider, within the bound.
A program may use at most 192 MiB of HBM per device.

v0:
```python
import jax
import jax.numpy as jnp
import numpy as np
from jax import lax
from jax.sharding import PartitionSpec as P

H = 16
HD = 64
MIDDLE_DILATION = 4
OUTER_DILATION = 32


VOID_LEVEL = -1e30


def partner(block, axis, stride):
    count = lax.axis_size(axis)
    route = []
    for low in range(count):
        high = low | 1 << stride
        if high != low and high < count:
            route += [(low, high), (high, low)]
    return lax.ppermute(block, axis, route)


def attend_one(query, keys, values):
    factor = query.shape[-1] ** (-0.5)
    scores = jnp.einsum("qd,kd->qk", query, keys, preferred_element_type=jnp.float32) * factor
    peak = jnp.max(scores, axis=-1, keepdims=True)
    powers = jnp.exp(scores - peak)
    total = jnp.sum(powers, axis=-1, keepdims=True)
    mixed = (
        jnp.einsum(
            "qk,kd->qd", powers.astype(jnp.bfloat16), values, preferred_element_type=jnp.float32
        )
        / total
    )
    return (mixed.astype(jnp.bfloat16), peak[:, 0] + jnp.log(total[:, 0]))


def attend_per_head(query, keys, values):
    return lax.map(
        lambda triple: attend_one(triple[0], triple[1], triple[2]), (query, keys, values)
    )


def to_heads(array):
    length = array.shape[0]
    return array.reshape(length, H, HD).transpose(1, 0, 2)


def dilate_tokens(array, rate):
    heads, length, depth = array.shape
    offsets = np.arange(heads) % rate
    return array.reshape(heads, length // rate, rate, depth)[np.arange(heads), :, offsets, :]


def spread_back(mixed, level, rate):
    heads, count, depth = mixed.shape
    chosen = np.arange(rate)[None, :] == (np.arange(heads) % rate)[:, None]
    full_out = (
        mixed.astype(jnp.float32)[:, :, None, :] * chosen.astype(np.float32)[:, None, :, None]
    ).reshape(heads, count * rate, depth)
    full_level = jnp.where(chosen[:, None, :], level[:, :, None], VOID_LEVEL).reshape(
        heads, count * rate
    )
    return (full_out, full_level)


def combine_levels(branches):
    peak = branches[0][1]
    for entry in branches[1:]:
        peak = jnp.maximum(peak, entry[1])
    numer = jnp.zeros(branches[0][0].shape, jnp.float32)
    denom = jnp.zeros(peak.shape, jnp.float32)
    for entry in branches:
        weight = jnp.exp(entry[1] - peak)
        numer = numer + weight[..., None] * entry[0].astype(jnp.float32)
        denom = denom + weight
    return numer / denom[..., None]


def per_device(queries, keys, values):
    row_count = queries.shape[0]
    query_per_head = to_heads(queries)
    key_per_head = to_heads(keys)
    value_per_head = to_heads(values)
    pair_key, pair_value = partner((key_per_head, value_per_head), "seq", 0)
    local_output, local_level = attend_per_head(
        query_per_head,
        jnp.concatenate([key_per_head, pair_key], axis=1),
        jnp.concatenate([value_per_head, pair_value], axis=1),
    )
    central_query = dilate_tokens(query_per_head, MIDDLE_DILATION)
    central_key = dilate_tokens(key_per_head, MIDDLE_DILATION)
    central_value = dilate_tokens(value_per_head, MIDDLE_DILATION)
    distant_query = dilate_tokens(query_per_head, OUTER_DILATION)
    total_bits = lax.axis_size("seq").bit_length() - 1
    group_bits = min(4, total_bits)
    group_key, group_value = (central_key, central_value)
    for bit_pos in range(group_bits):
        got_key, got_value = partner((group_key, group_value), "seq", bit_pos)
        group_key = jnp.concatenate([group_key, got_key], axis=1)
        group_value = jnp.concatenate([group_value, got_value], axis=1)
    central_output, central_level = attend_per_head(central_query, group_key, group_value)
    selected = np.arange(H) // MIDDLE_DILATION
    ratio = OUTER_DILATION // MIDDLE_DILATION
    all_key = group_key.reshape(H, -1, ratio, HD)[np.arange(H), :, selected, :]
    all_value = group_value.reshape(H, -1, ratio, HD)[np.arange(H), :, selected, :]
    for bit_pos in range(group_bits, total_bits):
        got_key, got_value = partner((all_key, all_value), "seq", bit_pos)
        all_key = jnp.concatenate([all_key, got_key], axis=1)
        all_value = jnp.concatenate([all_value, got_value], axis=1)
    distant_output, distant_level = attend_per_head(distant_query, all_key, all_value)
    merged_output = combine_levels(
        [
            (local_output, local_level),
            spread_back(central_output, central_level, MIDDLE_DILATION),
            spread_back(distant_output, distant_level, OUTER_DILATION),
        ]
    )
    far_rows = distant_output.transpose(1, 0, 2).reshape(row_count // OUTER_DILATION, H * HD)
    return (
        merged_output.transpose(1, 0, 2).reshape(row_count, H * HD).astype(jnp.bfloat16),
        far_rows,
    )


def solution(mesh):
    return jax.shard_map(
        per_device,
        mesh=mesh,
        in_specs=(P(("dp", "seq"), None), P(("dp", "seq"), None), P(("dp", "seq"), None)),
        out_specs=(P(("dp", "seq"), None), P(("dp", "seq"), None)),
        check_vma=False,
    )
```

profile of v0, /device:TPU:0, one launch (start us, length us, event | category | flops | bytes accessed | tf_op | source)
XLA Modules:
  0.0 468.7 jit_solution(17725890251183223965)
XLA Ops:
  10.3 6.2 %copy.101 = bf16[16,1024,64]{2,0,1:T(8,128)(2,1)} copy(bf16[16,1024,64]{1,2,0:T(8,128)(2,1)} %bitcast.21) | data formatting | bytes 4194304 | tf_op jit(solution)/shard_map/transpose | solution.py:49
  22.2 6.2 %copy.99 = bf16[16,1024,64]{2,0,1:T(8,128)(2,1)} copy(bf16[16,1024,64]{1,2,0:T(8,128)(2,1)} %bitcast.18) | data formatting | bytes 4194304 | tf_op jit(solution)/shard_map/transpose | solution.py:49
  36.1 29.6 %collective-permute-done.5 = bf16[16,256,64]{1,2,0:T(8,128)(2,1)} collective-permute-done((bf16[16,256,64]{1,2,0:T(8,128)(2,1)S(1)}, bf16[16,256,64]{1,2,0:T(8,128)(2,1)}, u32[]{:S(2)}, u32[]{:S(2)}) %collective-permute-start.5) | collective-permute-done | bytes 524320 | tf_op jit(solution)/shard_map/ppermute | solution.py:23
  70.0 6.9 %collective-permute-done.2 = bf16[16,256,64]{1,2,0:T(8,128)(2,1)S(1)} collective-permute-done((bf16[16,256,64]{1,2,0:T(8,128)(2,1)S(1)}, bf16[16,256,64]{1,2,0:T(8,128)(2,1)S(1)}, u32[]{:S(2)}, u32[]{:S(2)}) %collective-permute-start.2) | collective-permute-done | bytes 524320 | tf_op jit(solution)/shard_map/ppermute | solution.py:23
  91.8 5.9 %copy.109 = bf16[16,32,32,64]{3,1,2,0:T(8,128)(2,1)} copy(bf16[16,32,32,64]{3,2,1,0:T(8,128)(2,1)} %bitcast.129) | data formatting | bytes 4194304 | tf_op jit(solution)/shard_map/reshape | solution.py:55
  112.5 5.8 %collective-permute-done.3 = bf16[16,512,64]{1,2,0:T(8,128)(2,1)} collective-permute-done((bf16[16,512,64]{1,2,0:T(8,128)(2,1)}, bf16[16,512,64]{1,2,0:T(8,128)(2,1)}, u32[]{:S(2)}, u32[]{:S(2)}) %collective-permute-start.3) | collective-permute-done | bytes 1048608 | tf_op jit(solution)/shard_map/ppermute | solution.py:23
  132.0 180.9 %while.36 = (s32[]{:T(128)}, bf16[16,1024,64]{1,2,0:T(8,128)(2,1)}, f32[16,1024]{1,0:T(8,128)S(1)}, bf16[16,1024,64]{2,1,0:T(8,128)(2,1)}, bf16[16,2048,64]{1,2,...) while((s32[]{:T(128)}, bf16[16,1024,64]{1,2,0:T(8,128)(2,1)}, ...), condition=%wide.region_3.4_spmd, body=%wide.region_0.3_spmd.sunk | while | flops 553778176 | bytes 59680884 | solution.py:42
  160.3 5.7 %fusion.85 = bf16[16,1024,64]{1,2,0:T(8,128)(2,1)} fusion(bf16[16,1024,64]{1,2,0:T(8,128)(2,1)} %get-tuple-element.369, s32[]{:T(128)} %get-tuple-element.368, f32[1024,2048]{1,0:T(8,128)} %copy-done, f32[1024]{0:T(1024)S(1)} %get-tuple-element.319, bf16[16,2048,64]{1,2,0:T(8,128)(2,1)} %get-tuple-element.381, f32[1024]{0:T(1024)S(1)} %fusion.84), kind=kOutput, calls=%fused_computation.14.clone.1 | convolution fusion | flops 274857984 | bytes 8791040 | tf_op jit(solution)/shard_map/while/body/eval_jaxpr/qk,kd->qd/dot_general | solution.py:33
  182.9 5.7 %fusion.85 = bf16[16,1024,64]{1,2,0:T(8,128)(2,1)} fusion(bf16[16,1024,64]{1,2,0:T(8,128)(2,1)} %get-tuple-element.369, s32[]{:T(128)} %get-tuple-element.368, f32[1024,2048]{1,0:T(8,128)} %copy-done, f32[1024]{0:T(1024)S(1)} %get-tuple-element.319, bf16[16,2048,64]{1,2,0:T(8,128)(2,1)} %get-tuple-element.381, f32[1024]{0:T(1024)S(1)} %fusion.84), kind=kOutput, calls=%fused_computation.14.clone.1 | convolution fusion | flops 274857984 | bytes 8791040 | tf_op jit(solution)/shard_map/while/body/eval_jaxpr/qk,kd->qd/dot_general | solution.py:33
  194.2 5.7 %fusion.85 = bf16[16,1024,64]{1,2,0:T(8,128)(2,1)} fusion(bf16[16,1024,64]{1,2,0:T(8,128)(2,1)} %get-tuple-element.369, s32[]{:T(128)} %get-tuple-element.368, f32[1024,2048]{1,0:T(8,128)} %copy-done, f32[1024]{0:T(1024)S(1)} %get-tuple-element.319, bf16[16,2048,64]{1,2,0:T(8,128)(2,1)} %get-tuple-element.381, f32[1024]{0:T(1024)S(1)} %fusion.84), kind=kOutput, calls=%fused_computation.14.clone.1 | convolution fusion | flops 274857984 | bytes 8791040 | tf_op jit(solution)/shard_map/while/body/eval_jaxpr/qk,kd->qd/dot_general | solution.py:33
  228.1 5.7 %fusion.85 = bf16[16,1024,64]{1,2,0:T(8,128)(2,1)} fusion(bf16[16,1024,64]{1,2,0:T(8,128)(2,1)} %get-tuple-element.369, s32[]{:T(128)} %get-tuple-element.368, f32[1024,2048]{1,0:T(8,128)} %copy-done, f32[1024]{0:T(1024)S(1)} %get-tuple-element.319, bf16[16,2048,64]{1,2,0:T(8,128)(2,1)} %get-tuple-element.381, f32[1024]{0:T(1024)S(1)} %fusion.84), kind=kOutput, calls=%fused_computation.14.clone.1 | convolution fusion | flops 274857984 | bytes 8791040 | tf_op jit(solution)/shard_map/while/body/eval_jaxpr/qk,kd->qd/dot_general | solution.py:33
  239.4 5.7 %fusion.85 = bf16[16,1024,64]{1,2,0:T(8,128)(2,1)} fusion(bf16[16,1024,64]{1,2,0:T(8,128)(2,1)} %get-tuple-element.369, s32[]{:T(128)} %get-tuple-element.368, f32[1024,2048]{1,0:T(8,128)} %copy-done, f32[1024]{0:T(1024)S(1)} %get-tuple-element.319, bf16[16,2048,64]{1,2,0:T(8,128)(2,1)} %get-tuple-element.381, f32[1024]{0:T(1024)S(1)} %fusion.84), kind=kOutput, calls=%fused_computation.14.clone.1 | convolution fusion | flops 274857984 | bytes 8791040 | tf_op jit(solution)/shard_map/while/body/eval_jaxpr/qk,kd->qd/dot_general | solution.py:33
  250.8 5.7 %fusion.85 = bf16[16,1024,64]{1,2,0:T(8,128)(2,1)} fusion(bf16[16,1024,64]{1,2,0:T(8,128)(2,1)} %get-tuple-element.369, s32[]{:T(128)} %get-tuple-element.368, f32[1024,2048]{1,0:T(8,128)} %copy-done, f32[1024]{0:T(1024)S(1)} %get-tuple-element.319, bf16[16,2048,64]{1,2,0:T(8,128)(2,1)} %get-tuple-element.381, f32[1024]{0:T(1024)S(1)} %fusion.84), kind=kOutput, calls=%fused_computation.14.clone.1 | convolution fusion | flops 274857984 | bytes 8791040 | tf_op jit(solution)/shard_map/while/body/eval_jaxpr/qk,kd->qd/dot_general | solution.py:33
  273.4 5.7 %fusion.85 = bf16[16,1024,64]{1,2,0:T(8,128)(2,1)} fusion(bf16[16,1024,64]{1,2,0:T(8,128)(2,1)} %get-tuple-element.369, s32[]{:T(128)} %get-tuple-element.368, f32[1024,2048]{1,0:T(8,128)} %copy-done, f32[1024]{0:T(1024)S(1)} %get-tuple-element.319, bf16[16,2048,64]{1,2,0:T(8,128)(2,1)} %get-tuple-element.381, f32[1024]{0:T(1024)S(1)} %fusion.84), kind=kOutput, calls=%fused_computation.14.clone.1 | convolution fusion | flops 274857984 | bytes 8791040 | tf_op jit(solution)/shard_map/while/body/eval_jaxpr/qk,kd->qd/dot_general | solution.py:33
  284.7 5.7 %fusion.85 = bf16[16,1024,64]{1,2,0:T(8,128)(2,1)} fusion(bf16[16,1024,64]{1,2,0:T(8,128)(2,1)} %get-tuple-element.369, s32[]{:T(128)} %get-tuple-element.368, f32[1024,2048]{1,0:T(8,128)} %copy-done, f32[1024]{0:T(1024)S(1)} %get-tuple-element.319, bf16[16,2048,64]{1,2,0:T(8,128)(2,1)} %get-tuple-element.381, f32[1024]{0:T(1024)S(1)} %fusion.84), kind=kOutput, calls=%fused_computation.14.clone.1 | convolution fusion | flops 274857984 | bytes 8791040 | tf_op jit(solution)/shard_map/while/body/eval_jaxpr/qk,kd->qd/dot_general | solution.py:33
  307.3 5.7 %fusion.85 = bf16[16,1024,64]{1,2,0:T(8,128)(2,1)} fusion(bf16[16,1024,64]{1,2,0:T(8,128)(2,1)} %get-tuple-element.369, s32[]{:T(128)} %get-tuple-element.368, f32[1024,2048]{1,0:T(8,128)} %copy-done, f32[1024]{0:T(1024)S(1)} %get-tuple-element.319, bf16[16,2048,64]{1,2,0:T(8,128)(2,1)} %get-tuple-element.381, f32[1024]{0:T(1024)S(1)} %fusion.84), kind=kOutput, calls=%fused_computation.14.clone.1 | convolution fusion | flops 274857984 | bytes 8791040 | tf_op jit(solution)/shard_map/while/body/eval_jaxpr/qk,kd->qd/dot_general | solution.py:33
  313.0 6.2 %copy.117 = bf16[16,1024,64]{2,0,1:T(8,128)(2,1)} copy(bf16[16,1024,64]{1,2,0:T(8,128)(2,1)} %get-tuple-element.104) | data formatting | bytes 4194304 | tf_op jit(solution)/shard_map/while | solution.py:42
  322.8 8.4 %copy.105 = bf16[16,2048,64]{2,1,0:T(8,128)(2,1)} copy(bf16[16,2048,64]{1,2,0:T(8,128)(2,1)} %pad_maximum_fusion.3) | data formatting | bytes 8388608 | tf_op jit(solution)/shard_map/while | solution.py:42
  331.2 9.1 %copy.113 = bf16[16,256,8,64]{1,3,2,0:T(8,128)(2,1)} copy(bf16[16,256,8,64]{3,2,1,0:T(8,128)(2,1)} %bitcast.126) | data formatting | bytes 8388608 | tf_op jit(solution)/shard_map/reshape | solution.py:109
  343.9 8.4 %copy.104 = bf16[16,2048,64]{2,1,0:T(8,128)(2,1)} copy(bf16[16,2048,64]{1,2,0:T(8,128)(2,1)} %pad_maximum_fusion.2) | data formatting | bytes 8388608 | tf_op jit(solution)/shard_map/while | solution.py:42
  352.3 9.1 %copy.111 = bf16[16,256,8,64]{1,3,2,0:T(8,128)(2,1)} copy(bf16[16,256,8,64]{3,2,1,0:T(8,128)(2,1)} %bitcast.127) | data formatting | bytes 8388608 | tf_op jit(solution)/shard_map/reshape | solution.py:108
  367.1 11.2 %while.38 = (s32[]{:T(128)}, bf16[16,32,64]{2,1,0:T(8,128)(2,1)S(1)}, f32[16,32]{1,0:T(8,128)S(1)}, bf16[16,32,64]{2,1,0:T(8,128)(2,1)S(1)}, bf16[16,256,64]{1,2...) while((s32[]{:T(128)}, bf16[16,32,64]{2,1,0:T(8,128)(2,1)S(1)}, ...), condition=%wide.region_11.12_spmd, body=%wide.region_8.11_spmd.sunk | while | flops 2150370 | bytes 184409 | solution.py:42
  378.6 59.3 %while.37 = (s32[]{:T(128)}, bf16[16,256,64]{1,2,0:T(8,128)(2,1)S(1)}, f32[16,256]{1,0:T(8,128)S(1)}, bf16[16,256,64]{1,2,0:T(8,128)(2,1)}, bf16[16,2048,64]{2,1...) while((s32[]{:T(128)}, bf16[16,256,64]{1,2,0:T(8,128)(2,1)S(1)}, ...), condition=%wide.region_7.8_spmd, body=%wide.region_4.7_spmd.sunk | while | flops 137395968 | bytes 7417945 | solution.py:42
  445.7 15.2 %fusion.61 = bf16[16,1024,64]{2,0,1:T(8,128)(2,1)} fusion(f32[16,1024,64]{2,1,0:T(8,128)S(1)} %bitcast.128, bf16[16,1024,64]{2,0,1:T(8,128)(2,1)S(1)} %copy-done.1, f32[16,1024]{0,1:T(8,128)S(1)} %copy-done.5, f32[16,1024]{0,1:T(8,128)S(1)} %bitcast.138, f32[16,1024]{0,1:T(8,128)S(1)} %copy-done.4, f32[16,1024]{0,1:T(8,128)S(1)} %bitcast.137, ...), kind=kLoop, calls=%fused_computation.69 | loop fusion | flops 10485760 | bytes 9830400 | tf_op jit(solution)/shard_map/convert_element_type | solution.py:124
  (351 shorter events, 298.6 us)
Async XLA Ops:
  0.6 7.1 %copy-start.6 = (bf16[1024,1024]{1,0:T(8,128)(2,1)S(1)}, bf16[1024,1024]{1,0:T(8,128)(2,1)}, u32[]{:S(2)}) copy-start(bf16[1024,1024]{1,0:T(8,128)(2,1)} %param.38) | copy-start | bytes 6291460
  4.7 117.9 %collective-permute-start = (bf16[16,1024,64]{1,2,0:T(8,128)(2,1)}, bf16[16,1024,64]{1,2,0:T(8,128)(2,1)}, u32[]{:S(2)}, u32[]{:S(2)}) collective-permute-start(bf16[16,1024,64]{1,2,0:T(8,128)(2,1)} %bitcast.18), channel_id=1, source_target_pairs={{0,1},{1,0},{2,3},{3,2},{4,5},{5,4},{6,7},{7,6},{8,9},{9,8},{10,11... | collective-permute-start | bytes 6291464 | tf_op jit(solution)/shard_map/ppermute | solution.py:23
  16.5 5.0 %copy-start.7 = (s32[16]{0:T(128)S(1)}, s32[16]{0:T(128)}, u32[]{:S(2)}) copy-start(s32[16]{0:T(128)} %constant.194) | copy-start | bytes 196
  22.1 43.6 %collective-permute-start.5 = (bf16[16,256,64]{1,2,0:T(8,128)(2,1)S(1)}, bf16[16,256,64]{1,2,0:T(8,128)(2,1)}, u32[]{:S(2)}, u32[]{:S(2)}) collective-permute-start(bf16[16,256,64]{1,2,0:T(8,128)(2,1)S(1)} %gather_fusion.2), channel_id=1, source_target_pairs={{0,1},{1,0},{2,3},{3,2},{4,5},{5,4},{6,7},{7,6},{8,9},{9,8},{10,11... | collective-permute-start | bytes 1572872 | tf_op jit(solution)/shard_map/ppermute | solution.py:23
  34.0 42.9 %collective-permute-start.2 = (bf16[16,256,64]{1,2,0:T(8,128)(2,1)S(1)}, bf16[16,256,64]{1,2,0:T(8,128)(2,1)S(1)}, u32[]{:S(2)}, u32[]{:S(2)}) collective-permute-start(bf16[16,256,64]{1,2,0:T(8,128)(2,1)S(1)} %gather_fusion.1), channel_id=1, source_target_pairs={{0,1},{1,0},{2,3},{3,2},{4,5},{5,4},{6,7},{7,6},{8,9},{9,8},{10,11... | collective-permute-start | bytes 1572872 | tf_op jit(solution)/shard_map/ppermute | solution.py:23
  36.0 91.3 %collective-permute-start.1 = (bf16[16,1024,64]{1,2,0:T(8,128)(2,1)}, bf16[16,1024,64]{1,2,0:T(8,128)(2,1)}, u32[]{:S(2)}, u32[]{:S(2)}) collective-permute-start(bf16[16,1024,64]{1,2,0:T(8,128)(2,1)} %bitcast.21), channel_id=1, source_target_pairs={{0,1},{1,0},{2,3},{3,2},{4,5},{5,4},{6,7},{7,6},{8,9},{9,8},{10,11... | collective-permute-start | bytes 6291464 | tf_op jit(solution)/shard_map/ppermute | solution.py:23
  67.9 39.1 %collective-permute-start.6 = (bf16[16,512,64]{1,2,0:T(8,128)(2,1)}, bf16[16,512,64]{1,2,0:T(8,128)(2,1)}, u32[]{:S(2)}, u32[]{:S(2)}) collective-permute-start(bf16[16,512,64]{1,2,0:T(8,128)(2,1)} %pad_maximum_fusion.7), channel_id=1, source_target_pairs={{0,2},{2,0},{1,3},{3,1},{4,6},{6,4},{5,7},{7,5},{8,10},{10,8},{9,1... | collective-permute-start | bytes 3145736 | tf_op jit(solution)/shard_map/ppermute | solution.py:23
  78.7 39.6 %collective-permute-start.3 = (bf16[16,512,64]{1,2,0:T(8,128)(2,1)}, bf16[16,512,64]{1,2,0:T(8,128)(2,1)}, u32[]{:S(2)}, u32[]{:S(2)}) collective-permute-start(bf16[16,512,64]{1,2,0:T(8,128)(2,1)} %pad_maximum_fusion.6), channel_id=1, source_target_pairs={{0,2},{2,0},{1,3},{3,1},{4,6},{6,4},{5,7},{7,5},{8,10},{10,8},{9,1... | collective-permute-start | bytes 3145736 | tf_op jit(solution)/shard_map/ppermute | solution.py:23
  104.1 14.2 %copy-start.3 = (bf16[16,256,64]{1,2,0:T(8,128)(2,1)S(1)}, bf16[16,256,64]{1,2,0:T(8,128)(2,1)}, u32[]{:S(2)}) copy-start(bf16[16,256,64]{1,2,0:T(8,128)(2,1)} %copy-done.2) | copy-start | bytes 1572868
  109.9 209.2 %collective-permute-start.7 = (bf16[16,1024,64]{1,2,0:T(8,128)(2,1)}, bf16[16,1024,64]{1,2,0:T(8,128)(2,1)}, u32[]{:S(2)}, u32[]{:S(2)}) collective-permute-start(bf16[16,1024,64]{1,2,0:T(8,128)(2,1)} %pad_maximum_fusion.5), channel_id=1, source_target_pairs={{0,4},{4,0},{1,5},{5,1},{2,6},{6,2},{3,7},{7,3},{8,12},{12,8},{9,1... | collective-permute-start | bytes 6291464 | tf_op jit(solution)/shard_map/ppermute | solution.py:23
  121.2 219.1 %collective-permute-start.4 = (bf16[16,1024,64]{1,2,0:T(8,128)(2,1)}, bf16[16,1024,64]{1,2,0:T(8,128)(2,1)}, u32[]{:S(2)}, u32[]{:S(2)}) collective-permute-start(bf16[16,1024,64]{1,2,0:T(8,128)(2,1)} %pad_maximum_fusion.4), channel_id=1, source_target_pairs={{0,4},{4,0},{1,5},{5,1},{2,6},{6,2},{3,7},{7,3},{8,12},{12,8},{9,1... | collective-permute-start | bytes 6291464 | tf_op jit(solution)/shard_map/ppermute | solution.py:23
  145.7 3.2 copy-start
  157.0 3.2 copy-start
  179.6 3.2 copy-start
  190.9 3.2 copy-start
  202.2 3.2 copy-start
  213.5 3.2 copy-start
  224.8 3.2 copy-start
  236.1 3.2 copy-start
  247.4 3.2 copy-start
  352.3 9.1 %copy-start.8 = (s32[16]{0:T(128)S(1)}, s32[16]{0:T(128)}, u32[]{:S(2)}) copy-start(s32[16]{0:T(128)} %constant.218) | copy-start | bytes 196
  361.4 16.9 %copy-start.13 = (pred[16,32]{1,0:T(8,128)(4,1)S(1)}, pred[16,32]{1,0:T(8,128)(4,1)}, u32[]{:S(2)}) copy-start(pred[16,32]{1,0:T(8,128)(4,1)} %constant.104) | copy-start | bytes 1540
  361.4 17.2 %copy-start.9 = (bf16[16,256,64]{1,2,0:T(8,128)(2,1)S(1)}, bf16[16,256,64]{1,2,0:T(8,128)(2,1)}, u32[]{:S(2)}) copy-start(bf16[16,256,64]{1,2,0:T(8,128)(2,1)} %custom-call.14) | copy-start | bytes 1572868
  378.6 59.4 %copy-start.14 = (pred[16,4]{0,1:T(4,128)(4,1)S(1)}, pred[16,4]{0,1:T(4,128)(4,1)}, u32[]{:S(2)}) copy-start(pred[16,4]{0,1:T(4,128)(4,1)} %constant.101) | copy-start | bytes 196
  (14 other events, 32.5 us)
where the time goes:
time: 472 us; the launch traced here: 469 us
  matrix products  186 us (39%)
  local copies, waits for them, and re-layouts  142 us (30%)
  other arithmetic  82.5 us (17%)
  waiting for transfers between devices  42.3 us (9%)
  starting transfers between devices  13.5 us (3%)
    dot_general x48, matrix products, attend_one(): jnp.einsum('qk,kd->qd', powers.astype(jnp.bfloat16), values, preferred_el...  119 us
    dot_general x48, matrix products, attend_one(): jnp.einsum('qd,kd->qk', query, keys, preferred_element_type=jnp.float32)  66.9 us
    ppermute x8, waiting for transfers between devices, partner(): return lax.ppermute(block, axis, route)  42.3 us
    reduce_sum x48, other arithmetic, attend_one(): total = jnp.sum(powers, axis=-1, keepdims=True)  41.1 us
    while x5, local copies, waits for them, and re-layouts, attend_per_head(): lax.map(lambda triple: attend_one(triple[0], triple[1], triple[2]), (quer...  26.3 us
    reshape x4, local copies, waits for them, and re-layouts, dilate_tokens(): array.reshape(heads, length // rate, rate, depth)  20.9 us
    while x32, local copies, waits for them, and re-layouts  20.3 us
    transpose x3, local copies, waits for them, and re-layouts, to_heads(): return array.reshape(length, H, HD).transpose(1, 0, 2)  17.3 us
  transfers between devices with their start and end apart: 8, of which 3 were waited for; matrix products, arithmetic and copies ran while one was open for 55% of the time, Pallas kernels for 0%

commit v1 on v0

v1 whole, which is shorter than its diff:
```python
import functools

import jax
import jax.numpy as jnp
from jax import lax
from jax.experimental import pallas as pl
from jax.experimental.pallas import tpu as pltpu
from jax.sharding import PartitionSpec as P

H = 16
HD = 64
MID = 4
FAR = 32
GROUP = 16
LOG2E = 1.4426950408889634
NT = (((1,), (1,)), ((), ()))


def pick_rows(array, rate, want):
    rows, cols = array.shape
    head = jnp.arange(cols) % (H * HD) // HD
    keep = jnp.arange(rate)[:, None] == want(head)[None, :]
    parts = array.reshape(rows // rate, rate, cols)
    return jnp.sum(jnp.where(keep[None], parts, jnp.zeros((), array.dtype)), axis=1)


def soft_step(q, k, v_ones, m, acc, factor):
    s = lax.dot_general(q, k, NT, preferred_element_type=jnp.float32)
    top = jnp.max(s, axis=1, keepdims=True)
    m_new = top if m is None else jnp.maximum(m, top)
    e = jnp.exp2((s - m_new) * factor).astype(jnp.bfloat16)
    part = jnp.dot(e, v_ones, preferred_element_type=jnp.float32)
    if m is None:
        return m_new, part
    return m_new, acc * jnp.exp2((m - m_new) * factor) + part


def attend_kernel(factor, tk, perm_ref, back_ref, q_ref, k_ref, v_ref, pk_ref, pv_ref, mk_ref, mv_ref,
                  fk_ref, fv_ref, out_ref, far_ref, qp, acc, mx, rows_out):
    pair = pl.program_id(0)
    n_rows = q_ref.shape[0]
    block = n_rows // MID
    sub = n_rows // FAR
    qp[...] = jnp.dot(perm_ref[...], q_ref[...], preferred_element_type=jnp.float32).astype(jnp.bfloat16)

    def with_ones(v):
        return jnp.concatenate([v, jnp.ones_like(v)], axis=1)

    for side in range(2):
        head = pair * 2 + side
        lane = lax.broadcasted_iota(jnp.int32, (1, 2 * HD), 1)
        mine = lane // HD == side

        def masked(q):
            return jnp.where(mine, q, jnp.zeros_like(q))

        def near(tile, _):
            rows = pl.ds(pl.multiple_of(tile * block, block), block)
            q = masked(qp[rows, :])
            m, a = None, None
            for kr, vr in ((k_ref, v_ref), (pk_ref, pv_ref)):
                for at in range(0, n_rows, tk):
                    m, a = soft_step(q, kr[at:at + tk, :], with_ones(vr[at:at + tk, :]), m, a, factor)
            acc[rows, :] = a
            mx[rows, :] = jnp.broadcast_to(m, (block, 2 * HD))
            return 0

        lax.fori_loop(0, MID, near, 0)
        base = pl.multiple_of(lax.rem(head, MID) * block, block)
        rows = pl.ds(base, block)
        q = masked(qp[rows, :])
        m, a = mx[rows, 0:1], acc[rows, :]
        for at in range(0, mk_ref.shape[0], tk):
            m, a = soft_step(q, mk_ref[at:at + tk, :], with_ones(mv_ref[at:at + tk, :]), m, a, factor)
        acc[rows, :] = a
        mx[rows, :] = jnp.broadcast_to(m, (block, 2 * HD))
        rows = pl.ds(pl.multiple_of(base + (head // MID) * sub, sub), sub)
        q = masked(qp[rows, :])
        fm, fa = soft_step(q, fk_ref[...], with_ones(fv_ref[...]), None, None, factor)
        far = (fa[:, :2 * HD] / fa[:, 2 * HD:]).astype(jnp.bfloat16)
        m, a = mx[rows, 0:1], acc[rows, :]
        top = jnp.maximum(m, fm)
        acc[rows, :] = a * jnp.exp2((m - top) * factor) + fa * jnp.exp2((fm - top) * factor)
        res = (acc[:, :2 * HD] / acc[:, 2 * HD:]).astype(jnp.bfloat16)
        if side == 0:
            far_ref[...] = far
            rows_out[...] = res
        else:
            far_ref[...] = jnp.where(mine, far, far_ref[...])
            rows_out[...] = jnp.where(mine, res, rows_out[...])
    out_ref[...] = jnp.dot(back_ref[...], rows_out[...], preferred_element_type=jnp.float32).astype(jnp.bfloat16)


def per_device(queries, keys, values):
    n = lax.axis_size("seq")
    group = min(GROUP, n)
    rows = queries.shape[0]
    swap = [(i, i ^ 1) for i in range(n)]
    pk = lax.ppermute(keys, "seq", swap)
    pv = lax.ppermute(values, "seq", swap)
    kv = jnp.concatenate([keys, values], axis=1)
    own = pick_rows(kv, MID, lambda h: h % MID)
    sets = None if group == n else [list(range(g, g + group)) for g in range(0, n, group)]
    mids = lax.all_gather(own, "seq", axis_index_groups=sets, tiled=True)
    if group == n:
        fars = pick_rows(mids, FAR // MID, lambda h: h // MID)
    else:
        fars = lax.all_gather(pick_rows(own, FAR // MID, lambda h: h // MID), "seq", tiled=True)
    spot = jnp.arange(rows)
    token = spot % (rows // FAR) * FAR + spot // (rows // FAR) % (FAR // MID) * MID + spot // (rows // MID)
    perm = (token[:, None] == spot[None, :]).astype(jnp.bfloat16)
    back = (token[None, :] == spot[:, None]).astype(jnp.bfloat16)
    wide = 2 * HD
    pairs = H // 2
    whole = lambda r: pl.BlockSpec((r, rows), lambda i: (0, 0), pipeline_mode=pl.Buffered(1))
    cols = lambda r: pl.BlockSpec((r, wide), lambda i: (0, i))
    shift = lambda r: pl.BlockSpec((r, wide), lambda i: (0, i + pairs))
    mr, fr = mids.shape[0], fars.shape[0]
    return pl.pallas_call(
        functools.partial(attend_kernel, HD ** -0.5 * LOG2E, 1024),
        grid=(pairs,),
        out_shape=(
            jax.ShapeDtypeStruct((rows, H * HD), jnp.bfloat16),
            jax.ShapeDtypeStruct((rows // FAR, H * HD), jnp.bfloat16),
        ),
        in_specs=[whole(rows), whole(rows)] + [cols(rows)] * 5 + [cols(mr), shift(mr), cols(fr), shift(fr)],
        out_specs=(cols(rows), cols(rows // FAR)),
        scratch_shapes=[
            pltpu.VMEM((rows, wide), jnp.bfloat16),
            pltpu.VMEM((rows, 2 * wide), jnp.float32),
            pltpu.VMEM((rows, wide), jnp.float32),
            pltpu.VMEM((rows, wide), jnp.bfloat16),
        ],
        compiler_params=pltpu.CompilerParams(vmem_limit_bytes=56 << 20),
    )(perm, back, queries, keys, values, pk, pv, mids, mids, fars, fars)


def solution(mesh):
    spec = P(("dp", "seq"), None)
    return jax.shard_map(per_device, mesh=mesh, in_specs=(spec, spec, spec), out_specs=(spec, spec), check_vma=False)
```

time: 472 us -> 326 us (0.69)
  matrix products: 186 us -> 0 us
  local copies, waits for them, and re-layouts: 142 us -> 7.21 us
  waiting for transfers between devices: 42.3 us -> 170 us
  Pallas kernels: 0 us -> 107 us
  other arithmetic: 82.5 us -> 23.4 us
  between operations: 0.92 us -> 14.1 us
  starting transfers between devices: 13.5 us -> 3.15 us
    dot_general x96 -> x0, matrix products: 186 us -> none  [the longest x48 119 us: attend_one(): jnp.einsum('qk,kd->qd', powers.astype(jnp.bfloat16), values, preferred_el...]
    all_gather x0 -> x1, waiting for transfers between devices: none -> 170 us  [per_device(): mids = lax.all_gather(own, 'seq', axis_index_groups=sets, tiled=True)]
    pallas_call x0 -> x1, Pallas kernels: none -> 107 us  [per_device(): pl.pallas_call(functools.partial(attend_kernel, HD ** (-0.5) * LOG2E, 102...]
    while x37 -> x0, local copies, waits for them, and re-layouts: 46.7 us -> none  [the longest x5 26.3 us: attend_per_head(): lax.map(lambda triple: attend_one(triple[0], triple[1], triple[2]), (quer...]
    ppermute x8 -> x2, waiting for transfers between devices: 42.3 us -> 0.01 us  [the longest x1 0.01 us: per_device(): pk = lax.ppermute(keys, 'seq', swap)]
    reshape x7 -> x1, local copies, waits for them, and re-layouts: 39.9 us -> 7.2 us  [pick_rows(): parts = array.reshape(rows // rate, rate, cols)]
    reduce_sum x48 -> x2, other arithmetic: 41.1 us -> 16 us  [pick_rows(): jnp.sum(jnp.where(keep[None], parts, jnp.zeros((), array.dtype)), axis=1)]
    concatenate x9 -> x1, other arithmetic: 25.6 us -> 4.68 us  [per_device(): kv = jnp.concatenate([keys, values], axis=1)]
  transfers between devices with their start and end apart: 8 -> 3, of which waited for: 3 -> 1; matrix products, arithmetic and copies ran while one was open for 55% -> 3% of each run, Pallas kernels for 0% -> 0%
where the time goes in v1:
time: 326 us; the launch traced here: 325 us
  waiting for transfers between devices  170 us (52%)
  Pallas kernels  107 us (33%)
  other arithmetic  23.4 us (7%)
  between operations  14.1 us (4%)
  local copies, waits for them, and re-layouts  7.21 us (2%)
    all_gather x1, waiting for transfers between devices, per_device(): mids = lax.all_gather(own, 'seq', axis_index_groups=sets, tiled=True)  170 us
    pallas_call x1, Pallas kernels, per_device(): pl.pallas_call(functools.partial(attend_kernel, HD ** (-0.5) * LOG2E, 102...  107 us
    reduce_sum x2, other arithmetic, pick_rows(): jnp.sum(jnp.where(keep[None], parts, jnp.zeros((), array.dtype)), axis=1)  16 us
    reshape x1, local copies, waits for them, and re-layouts, pick_rows(): parts = array.reshape(rows // rate, rate, cols)  7.2 us
  transfers between devices with their start and end apart: 3, of which 1 were waited for; matrix products, arithmetic and copies ran while one was open for 3% of the time, Pallas kernels for 0%

profile of v1, /device:TPU:0, one launch (start us, length us, event | category | flops | bytes accessed | tf_op | source)
XLA Modules:
  0.0 325.2 jit_solution(16384031435747326936)
XLA Ops:
  7.2 0.0 all-gather.2.cloned.1.call-start
  7.3 4.7 %pad_maximum_fusion = bf16[1024,2048]{1,0:T(8,128)(2,1)} fusion(bf16[1024,1024]{1,0:T(8,128)(2,1)} %v_ref.1, bf16[1024,1024]{1,0:T(8,128)(2,1)} %k_ref.1), kind=kLoop, calls=%fused_computation.2 | loop fusion | flops 8388608 | bytes 8388608 | tf_op jit(solution)/shard_map/concatenate | solution.py:101
  11.9 7.2 %reshape.188 = bf16[256,4,2048]{2,1,0:T(4,128)(2,1)} reshape(bf16[1024,2048]{1,0:T(8,128)(2,1)} %pad_maximum_fusion) | data formatting | bytes 8388608 | tf_op jit(solution)/shard_map/reshape | solution.py:23
  19.1 0.0 copy-start
  19.1 7.6 %select_reduce_fusion = bf16[256,2048]{1,0:T(8,128)(2,1)} fusion(bf16[256,4,2048]{2,1,0:T(4,128)(2,1)} %reshape.188, pred[4,2048]{1,0:T(4,128)(4,1)S(1)} %iota_compare_fusion.3), kind=kLoop, calls=%fused_computation.3 | loop fusion | flops 3670016 | bytes 5251072 | tf_op jit(solution)/shard_map/reduce_sum | solution.py:24
  26.7 0.0 all-gather.2.cloned.1.call-update
  26.7 0.0 copy-done
  26.7 3.0 collective-permute-start
  29.8 0.1 collective-permute-start.1
  29.9 2.7 fusion.2
  32.6 170.4 %all-gather.2.cloned.1.call-done.mk_ref.mv_ref = bf16[2048,2048]{1,0:T(8,128)(2,1)} async-done(((bf16[256,2048]{1,0:T(8,128)(2,1)}), bf16[2048,2048]{1,0:T(8,128)(2,1)}) %all-gather.2.cloned.1.call-update) | async-done | bytes 8388624 | tf_op jit(solution)/shard_map/all_gather | solution.py:104
  202.9 8.4 %fusion.fk_ref.fv_ref = bf16[256,2048]{1,0:T(8,128)(2,1)} fusion(bf16[2048,2048]{1,0:T(8,128)(2,1)} %all-gather.2.cloned.1.call-done.mk_ref.mv_ref, pred[8,2048]{1,0:T(8,128)(4,1)S(1)} %iota_compare_fusion.2), kind=kLoop, calls=%fused_computation.1 | loop fusion | flops 7864320 | bytes 9453568 | tf_op jit(solution)/shard_map/reduce_sum | solution.py:24
  211.3 0.0 collective-permute-done.pk_ref
  211.3 0.0 collective-permute-done.1.pv_ref
  211.3 107.1 %shard_map.50 = (bf16[1024,1024]{1,0:T(8,128)(2,1)}, bf16[32,1024]{1,0:T(8,128)(2,1)}) custom-call(bf16[1024,1024]{1,0:T(8,128)(2,1)} %get-tuple-element.3.perm_ref, bf16[1024,1024]{1,0:T(8,128)(2,1)} %get-tuple-element.2.back_ref, bf16[1024,1024]{1,0:T(8,128)(2,1)} %q_ref.1, bf16[1024,1024]{1,0:T(8,128)(2,1)} %k_ref.1, bf16[1024,1024]{1,0:T(8,128)(2,1)} %v_ref.1, ...), custom_call_target="tpu_custom_call" | custom-call | tf_op jit(solution)/shard_map/pallas_call | solution.py:119
  (5 shorter events, 0.1 us)
Async XLA Ops:
  7.2 195.8 %all-gather.2.cloned.1.call-start = ((), (), s32[]{:S(2)}) async-start(), calls=%async_computation | async-start | bytes 9437184 | tf_op jit(solution)/shard_map/all_gather | solution.py:104
  19.1 7.6 %copy-start = (bf16[1024,1024]{1,0:T(8,128)(2,1)S(1)}, bf16[1024,1024]{1,0:T(8,128)(2,1)}, u32[]{:S(2)}) copy-start(bf16[1024,1024]{1,0:T(8,128)(2,1)} %k_ref.1) | copy-start | bytes 6291460
  26.7 184.6 %collective-permute-start = (bf16[1024,1024]{1,0:T(8,128)(2,1)S(1)}, bf16[1024,1024]{1,0:T(8,128)(2,1)}, u32[]{:S(2)}, u32[]{:S(2)}) collective-permute-start(bf16[1024,1024]{1,0:T(8,128)(2,1)S(1)} %copy-done), channel_id=1, source_target_pairs={{0,1},{1,0},{2,3},{3,2},{4,5},{5,4},{6,7},{7,6},{8,9},{9,8},{10,11... | collective-permute-start | bytes 6291464 | tf_op jit(solution)/shard_map/ppermute | solution.py:99
  29.8 181.5 %collective-permute-start.1 = (bf16[1024,1024]{1,0:T(8,128)(2,1)}, bf16[1024,1024]{1,0:T(8,128)(2,1)}, u32[]{:S(2)}, u32[]{:S(2)}) collective-permute-start(bf16[1024,1024]{1,0:T(8,128)(2,1)} %v_ref.1), channel_id=1, source_target_pairs={{0,1},{1,0},{2,3},{3,2},{4,5},{5,4},{6,7},{7,6},{8,9},{9,8},{10,11... | collective-permute-start | bytes 6291464 | tf_op jit(solution)/shard_map/ppermute | solution.py:100
Sparse Core Ops, SparseCore 0:
  26.9 176.0 all-gather.1

commit v2 on v1

v2 whole, which is shorter than its diff:
```python
import functools

import jax
import jax.numpy as jnp
from jax import lax
from jax.experimental import pallas as pl
from jax.experimental.pallas import tpu as pltpu
from jax.sharding import PartitionSpec as P

H = 16
HD = 64
MID = 4
FAR = 32
GROUP = 16
SUB = 16
TILE = SUB * FAR
BLOCK = TILE // MID
PAIRS = H // 2
WIDE = 2 * HD
CUTS = 4
PER_CUT = PAIRS // CUTS
CUT = WIDE * PER_CUT
ROWS = 256
FACTOR = HD ** -0.5 * 1.4426950408889634
NT = (((1,), (1,)), ((), ()))


def attend(q, k, v):
    s = lax.dot_general(q, k, NT, preferred_element_type=jnp.float32)
    m = jnp.max(s, axis=1, keepdims=True)
    e = jnp.exp2((s - m) * FACTOR).astype(jnp.bfloat16)
    part = jnp.dot(e, jnp.concatenate([v, jnp.ones_like(v)], axis=1), preferred_element_type=jnp.float32)
    return m, part[:, :WIDE], part[:, WIDE:]


def kernel(n, group, q_ref, k_ref, v_ref, out_ref, far_ref, pk, pv, mid, others, qp, num, den, top, perm, back,
           near_send, near_recv, mid_send, mid_recv, far_send, far_recv):
    rows = q_ref.shape[0]
    tiles = rows // TILE
    length = group // 2
    rounds = length - 2
    me = lax.axis_index("seq")
    base = me // group * group
    inside = lax.rem(me, group)
    side = lax.rem(inside, 2)
    pos = inside // 2
    partner = base + pos * 2 + 1 - side
    lane = lax.broadcasted_iota(jnp.int32, (1, WIDE), 1)
    first = lane < HD
    foreign = [lax.rem(base + group + i, n) for i in range(n - group)]

    def slot(at, u):
        return at * 2 + (side if u == 0 else 1 - side)

    def near_copy(cut, which):
        cols = pl.ds(cut * CUT, CUT)
        src, dst = ((k_ref, pk), (v_ref, pv))[which]
        return pltpu.make_async_remote_copy(
            src_ref=src.at[:, cols], dst_ref=dst.at[:, cols], send_sem=near_send.at[which, cut],
            recv_sem=near_recv.at[which, cut], device_id={"seq": partner}, device_id_type=pl.DeviceIdType.MESH)

    def line_copy(u, d, cut, right):
        at = slot(pos - d, u) if right else slot(pos + d, u)
        to = me + 2 if right else me - 2
        return pltpu.make_async_remote_copy(
            src_ref=mid.at[at, cut], dst_ref=mid.at[at, cut], send_sem=mid_send.at[int(right), u, d, cut],
            recv_sem=mid_recv.at[at, cut], device_id={"seq": to}, device_id_type=pl.DeviceIdType.MESH)

    def far_copy(i, arrived=False):
        there = foreign[i] // group * group
        at = i if arrived else lax.rem(me - there - group + 2 * n, n)
        return pltpu.make_async_remote_copy(
            src_ref=others.at[n - group], dst_ref=others.at[at], send_sem=far_send.at[i], recv_sem=far_recv.at[at],
            device_id={"seq": foreign[i]}, device_id_type=pl.DeviceIdType.MESH)

    def both(u, d, cut, act):
        @pl.when(jnp.logical_and(pos - d >= 0, pos < length - 1))
        def _():
            act(line_copy(u, d, cut, True))

        @pl.when(jnp.logical_and(pos + d < length, pos > 0))
        def _():
            act(line_copy(u, d, cut, False))

    def arrive(u, d, cut):
        @pl.when(pos - d >= 0)
        def _():
            line_copy(u, d, cut, True).wait_recv()

        @pl.when(pos + d < length)
        def _():
            line_copy(u, d, cut, False).wait_recv()

    def send(u, cut):
        both(u, 0, cut, lambda c: c.start())

    def relay(u, d, cut):
        arrive(u, d, cut)
        both(u, d, cut, lambda c: c.start())

    barrier = pltpu.get_barrier_semaphore()

    def greet(dev):
        pl.semaphore_signal(barrier, inc=1, device_id={"seq": dev}, device_id_type=pl.DeviceIdType.MESH)

    greet(partner)
    pl.when(pos > 0)(lambda: greet(me - 2))
    pl.when(pos < length - 1)(lambda: greet(me + 2))
    for dev in foreign:
        greet(dev)
    pl.semaphore_wait(barrier, 1 + len(foreign) + jnp.minimum(pos, 1) + jnp.minimum(length - 1 - pos, 1))

    for cut in range(CUTS):
        for which in range(2):
            near_copy(cut, which).start()

    def one_hot(spot, token):
        want = lax.rem(spot, SUB) * FAR + lax.rem(spot // SUB, FAR // MID) * MID + spot // BLOCK
        return jnp.where(want == token, 1.0, 0.0).astype(jnp.bfloat16)

    r = lax.broadcasted_iota(jnp.int32, (TILE, TILE), 0)
    c = lax.broadcasted_iota(jnp.int32, (TILE, TILE), 1)
    perm[...] = one_hot(r, c)
    back[...] = one_hot(c, r)

    def lanes_of(p):
        return pl.ds(pl.multiple_of(p * WIDE, WIDE), WIDE)

    def select(u, cut, keys, vals):
        def one(i, _):
            p = cut * PER_CUT + i
            at = pl.multiple_of(lax.rem(2 * p, MID) * BLOCK, 2 * BLOCK)
            pick = perm[pl.ds(at, 2 * BLOCK), :]
            for t in range(tiles):
                for which, ref in enumerate((keys, vals)):
                    got = jnp.dot(pick, ref[t * TILE:(t + 1) * TILE, lanes_of(p)], preferred_element_type=jnp.float32)
                    got = jnp.where(first, got[:BLOCK], got[BLOCK:]).astype(jnp.bfloat16)
                    mid[slot(pos, u), cut, t * BLOCK:(t + 1) * BLOCK, lanes_of(which * PER_CUT + i)] = got
            return 0

        lax.fori_loop(0, PER_CUT, one, 0)

    for cut in range(CUTS):
        select(0, cut, k_ref, v_ref)
        if cut:
            send(0, cut - 1)
    for t in range(tiles):
        span = slice(t * TILE, (t + 1) * TILE)
        for cut in range(CUTS):
            cols = slice(cut * CUT, (cut + 1) * CUT)
            qp[span, cols] = jnp.dot(perm[...], q_ref[span, cols], preferred_element_type=jnp.float32).astype(jnp.bfloat16)
    send(0, CUTS - 1)
    if n > group:
        for p in range(PAIRS):
            cut, i = divmod(p, PER_CUT)
            b = 2 * p // MID
            for t in range(tiles):
                for which in range(2):
                    cols = slice((which * PER_CUT + i) * WIDE, (which * PER_CUT + i + 1) * WIDE)
                    others[n - group, cut, t * SUB:(t + 1) * SUB, cols] = mid[
                        slot(pos, 0), cut, t * BLOCK + b * SUB:t * BLOCK + (b + 1) * SUB, cols]

    def merge(span, cols, mine, m, pn, pd):
        m0 = top[span, cols]
        t = jnp.maximum(m0, m)
        old, new = jnp.exp2((m0 - t) * FACTOR), jnp.exp2((m - t) * FACTOR)
        n1 = num[span, cols] * old + pn * new
        d1 = den[span, cols] * old + pd * new
        if mine is not None:
            t, n1, d1 = (jnp.where(mine, a, b[span, cols]) for a, b in ((t, top), (n1, num), (d1, den)))
        top[span, cols] = t
        num[span, cols] = n1
        den[span, cols] = d1

    def near(p, kr, vr, fresh):
        cols = lanes_of(p)

        def tile(i, _):
            span = pl.ds(pl.multiple_of(i * ROWS, ROWS), ROWS)
            q = qp[span, cols]
            k, v = kr[:, cols], vr[:, cols]
            ma, na, da = attend(jnp.where(first, q, jnp.zeros_like(q)), k, v)
            mb, nb, db = attend(jnp.where(first, jnp.zeros_like(q), q), k, v)
            m, pn, pd = jnp.where(first, ma, mb), jnp.where(first, na, nb), jnp.where(first, da, db)
            if fresh:
                top[span, cols] = m
                num[span, cols] = pn
                den[span, cols] = pd
            else:
                merge(span, cols, None, m, pn, pd)
            return 0

        lax.fori_loop(0, rows // ROWS, tile, 0)

    def middle(p, u):
        cols = lanes_of(p)
        cut, i = p // PER_CUT, lax.rem(p, PER_CUT)
        step = min(4, length)
        for at in range(0, length, step):
            k = jnp.concatenate([mid[slot(a, u), cut, :, lanes_of(i)] for a in range(at, at + step)], axis=0)
            v = jnp.concatenate([mid[slot(a, u), cut, :, lanes_of(i + PER_CUT)] for a in range(at, at + step)], axis=0)
            for s in range(2):
                mine = first if s == 0 else jnp.logical_not(first)
                spans = [pl.ds(pl.multiple_of(t * TILE + lax.rem(2 * p + s, MID) * BLOCK, BLOCK), BLOCK) for t in range(tiles)]
                q = jnp.concatenate([qp[x, cols] for x in spans], axis=0)
                m, pn, pd = attend(jnp.where(mine, q, jnp.zeros_like(q)), k, v)
                for t, x in enumerate(spans):
                    y = slice(t * BLOCK, (t + 1) * BLOCK)
                    merge(x, cols, mine, m[y], pn[y], pd[y])

    def far(p):
        cols = lanes_of(p)
        cut, i = p // PER_CUT, lax.rem(p, PER_CUT)
        b = 2 * p // MID

        def gather(j):
            got = [mid[a, cut, pl.ds(pl.multiple_of(t * BLOCK + b * SUB, SUB), SUB), lanes_of(j)]
                   for a in range(group) for t in range(tiles)]
            got += [others[a, cut, :, lanes_of(j)] for a in range(n - group)]
            return jnp.concatenate(got, axis=0)

        k, v = gather(i), gather(i + PER_CUT)
        kept = None
        for s in range(2):
            mine = first if s == 0 else jnp.logical_not(first)
            at = lax.rem(2 * p + s, MID) * BLOCK + b * SUB
            spans = [pl.ds(pl.multiple_of(t * TILE + at, SUB), SUB) for t in range(tiles)]
            q = jnp.concatenate([qp[x, cols] for x in spans], axis=0)
            m, pn, pd = attend(jnp.where(mine, q, jnp.zeros_like(q)), k, v)
            for t, x in enumerate(spans):
                y = slice(t * SUB, (t + 1) * SUB)
                merge(x, cols, mine, m[y], pn[y], pd[y])
            res = pn / pd
            kept = res if s == 0 else jnp.where(first, kept, res)
        far_ref[:, cols] = kept.astype(jnp.bfloat16)

    def take_near(cut):
        near_copy(cut, 0).wait_recv()
        near_copy(cut, 1).wait_recv()

    early = [(d, cut) for d in range(1, rounds + 1) for cut in range(CUTS)]
    share = -(-len(early) // PAIRS) if early else 0
    half = (rounds + 1) // 2
    low, high = range(1, half + 1), range(half + 1, rounds + 1)

    def phase_one(p, _):
        @pl.when(p == PAIRS - 3)
        def _():
            take_near(0)
            select(1, 0, pk, pv)

        near(p, k_ref, v_ref, True)
        for x in range(PAIRS):
            todo = early[x * share:(x + 1) * share]

            @pl.when(p == x)
            def _():
                for d, cut in todo:
                    relay(0, d, cut)

        @pl.when(p == PAIRS - 3)
        def _():
            send(1, 0)
        return 0

    lax.fori_loop(0, PAIRS, phase_one, 0)
    if n > group:
        for i in range(n - group):
            far_copy(i).start()
    gets = {0: 1, 3: 2, 6: 3}
    passes = {0: (low, 0), 1: (high, 0), 2: (low, 1), 3: (high, 1), 4: (low, 2), 5: (high, 2), 7: (low, 3)}

    def phase_two(p, _):
        for x, cut in gets.items():
            @pl.when(p == x)
            def _():
                take_near(cut)
                select(1, cut, pk, pv)

        for x in range(CUTS):
            @pl.when(p == x * PER_CUT)
            def _():
                if length > 1:
                    arrive(0, length - 1, x)

        near(p, pk, pv, False)
        middle(p, 0)
        for x in range(PAIRS):
            @pl.when(p == x)
            def _():
                if x in passes:
                    for d in passes[x][0]:
                        relay(1, d, passes[x][1])
                if x in gets:
                    send(1, gets[x])
        return 0

    lax.fori_loop(0, PAIRS, phase_two, 0)
    if n > group:
        for i in range(n - group):
            far_copy(i, True).wait_recv()

    def phase_three(p, _):
        for x in range(CUTS):
            @pl.when(p == x * PER_CUT)
            def _():
                if length > 1:
                    arrive(1, length - 1, x)

        middle(p, 1)
        far(p)
        cols = lanes_of(p)
        for t in range(tiles):
            span = slice(t * TILE, (t + 1) * TILE)
            res = (num[span, cols] / den[span, cols]).astype(jnp.bfloat16)
            out_ref[span, cols] = jnp.dot(back[...], res, preferred_element_type=jnp.float32).astype(jnp.bfloat16)

        @pl.when(p == 1)
        def _():
            for d in high:
                relay(1, d, CUTS - 1)
        return 0

    lax.fori_loop(0, PAIRS, phase_three, 0)
    for cut in range(CUTS):
        for which in range(2):
            near_copy(cut, which).wait_send()
        for u in range(2):
            for d in range(max(1, length - 1)):
                both(u, d, cut, lambda c: c.wait_send())
    for i in range(n - group):
        far_copy(i).wait_send()


def per_device(queries, keys, values):
    n = lax.axis_size("seq")
    group = min(GROUP, n)
    length = group // 2
    rows, cols = queries.shape
    spare = n - group
    dma = pltpu.SemaphoreType.DMA
    vmem = pl.BlockSpec(memory_space=pltpu.VMEM)
    return pl.pallas_call(
        functools.partial(kernel, n, group),
        out_shape=(
            jax.ShapeDtypeStruct((rows, cols), jnp.bfloat16),
            jax.ShapeDtypeStruct((rows // FAR, cols), jnp.bfloat16),
        ),
        in_specs=[vmem] * 3,
        out_specs=(vmem, vmem),
        scratch_shapes=[
            pltpu.VMEM((rows, cols), jnp.bfloat16),
            pltpu.VMEM((rows, cols), jnp.bfloat16),
            pltpu.VMEM((group, CUTS, rows // MID, 2 * CUT), jnp.bfloat16),
            pltpu.VMEM((spare + 1, CUTS, rows // FAR, 2 * CUT), jnp.bfloat16),
            pltpu.VMEM((rows, cols), jnp.bfloat16),
            pltpu.VMEM((rows, cols), jnp.float32),
            pltpu.VMEM((rows, cols), jnp.float32),
            pltpu.VMEM((rows, cols), jnp.float32),
            pltpu.VMEM((TILE, TILE), jnp.bfloat16),
            pltpu.VMEM((TILE, TILE), jnp.bfloat16),
            dma((2, CUTS)),
            dma((2, CUTS)),
            dma((2, 2, length, CUTS)),
            dma((group, CUTS)),
            dma((spare + 1,)),
            dma((spare + 1,)),
        ],
        compiler_params=pltpu.CompilerParams(collective_id=0, has_side_effects=True, vmem_limit_bytes=62 << 20),
    )(queries, keys, values)


def solution(mesh):
    spec = P(("dp", "seq"), None)
    return jax.shard_map(per_device, mesh=mesh, in_specs=(spec, spec, spec), out_specs=(spec, spec), check_vma=False)
```

time: 326 us -> 161 us (0.49)
  waiting for transfers between devices: 170 us -> 0 us
  Pallas kernels: 107 us -> 156 us
  other arithmetic: 23.4 us -> 0 us
  between operations: 14.1 us -> 0.65 us
  local copies, waits for them, and re-layouts: 7.21 us -> 3.75 us
    all_gather x1 -> x0, waiting for transfers between devices: 170 us -> none  [per_device(): mids = lax.all_gather(own, 'seq', axis_index_groups=sets, tiled=True)]
    pallas_call x1, Pallas kernels: 107 us -> 156 us  [per_device(): pl.pallas_call(functools.partial(kernel, n, group), out_shape=(jax.ShapeD...]
    reduce_sum x2 -> x0, other arithmetic: 16 us -> none  [pick_rows(): jnp.sum(jnp.where(keep[None], parts, jnp.zeros((), array.dtype)), axis=1)]
    reshape x1 -> x0, local copies, waits for them, and re-layouts: 7.2 us -> none  [pick_rows(): parts = array.reshape(rows // rate, rate, cols)]
    concatenate x1 -> x0, other arithmetic: 4.68 us -> none  [per_device(): kv = jnp.concatenate([keys, values], axis=1)]
    unnamed x2 -> x4, local copies, waits for them, and re-layouts: 0.01 us -> 3.75 us
  transfers between devices with their start and end apart: 3 -> 0, of which waited for: 1 -> 0; matrix products, arithmetic and copies ran while one was open for 3% -> 0% of each run, Pallas kernels for 0% -> 0%
where the time goes in v2:
time: 161 us
  Pallas kernels  156 us (97%)
  local copies, waits for them, and re-layouts  3.75 us (2%)
    pallas_call x1, Pallas kernels, per_device(): pl.pallas_call(functools.partial(kernel, n, group), out_shape=(jax.ShapeD...  156 us
    unnamed x4, local copies, waits for them, and re-layouts  3.75 us

profile of v2, /device:TPU:0, one launch (start us, length us, event | category | flops | bytes accessed | tf_op | source)
XLA Modules:
  0.0 160.6 jit_solution(215256944230728797)
XLA Ops:
  0.6 156.2 %shard_map.50 = (bf16[1024,1024]{1,0:T(8,128)(2,1)}, bf16[32,1024]{1,0:T(8,128)(2,1)}) custom-call(bf16[1024,1024]{1,0:T(8,128)(2,1)} %q_ref.1, bf16[1024,1024]{1,0:T(8,128)(2,1)} %k_ref.1, bf16[1024,1024]{1,0:T(8,128)(2,1)} %v_ref.1), custom_call_target="tpu_custom_call" | custom-call | tf_op jit(solution)/shard_map/pallas_call | solution.py:343
  156.8 0.0 copy-start
  156.8 3.1 %copy.7 = bf16[1024,1024]{1,0:T(8,128)(2,1)} copy(bf16[1024,1024]{1,0:T(8,128)(2,1)} %get-tuple-element.4) | data formatting | bytes 4194304
  160.0 0.0 copy-done
  160.0 0.6 copy.8
Async XLA Ops:
  156.8 3.1 %copy-start = (bf16[32,1024]{1,0:T(8,128)(2,1)S(1)}, bf16[32,1024]{1,0:T(8,128)(2,1)}, u32[]{:S(2)}) copy-start(bf16[32,1024]{1,0:T(8,128)(2,1)} %get-tuple-element.5) | copy-start | bytes 196612

commit v3 on v2

--- a/solution.py
+++ b/solution.py
@@ -34,7 +34,7 @@
 
 
 def kernel(n, group, q_ref, k_ref, v_ref, out_ref, far_ref, pk, pv, mid, others, qp, num, den, top, perm, back,
-           near_send, near_recv, mid_send, mid_recv, far_send, far_recv):
+           near_send, near_recv, mid_send, mid_recv, far_send, far_recv, cross_send):
     rows = q_ref.shape[0]
     tiles = rows // TILE
     length = group // 2
@@ -91,12 +91,24 @@
         def _():
             line_copy(u, d, cut, False).wait_recv()
 
+    def cross_copy(d, right):
+        at = slot(pos - d if right else pos + d, 0)
+        return pltpu.make_async_remote_copy(
+            src_ref=mid.at[at, CUTS - 1], dst_ref=mid.at[at, CUTS - 1], send_sem=cross_send.at[int(right), d],
+            recv_sem=mid_recv.at[at, CUTS - 1], device_id={"seq": partner}, device_id_type=pl.DeviceIdType.MESH)
+
+    def cross(d, act):
+        pl.when(pos - d >= 0)(lambda: act(cross_copy(d, True)))
+        pl.when(pos + d < length)(lambda: act(cross_copy(d, False)))
+
     def send(u, cut):
         both(u, 0, cut, lambda c: c.start())
 
     def relay(u, d, cut):
         arrive(u, d, cut)
         both(u, d, cut, lambda c: c.start())
+        if u == 0 and cut == CUTS - 1:
+            cross(d, lambda c: c.start())
 
     barrier = pltpu.get_barrier_semaphore()
 
@@ -190,7 +202,7 @@
                 merge(span, cols, None, m, pn, pd)
             return 0
 
-        lax.fori_loop(0, rows // ROWS, tile, 0)
+        lax.fori_loop(0, rows // ROWS, tile, 0, unroll=True)
 
     def middle(p, u):
         cols = lanes_of(p)
@@ -268,7 +280,7 @@
         for i in range(n - group):
             far_copy(i).start()
     gets = {0: 1, 3: 2, 6: 3}
-    passes = {0: (low, 0), 1: (high, 0), 2: (low, 1), 3: (high, 1), 4: (low, 2), 5: (high, 2), 7: (low, 3)}
+    passes = {0: (low, 0), 1: (high, 0), 2: (low, 1), 3: (high, 1), 4: (low, 2), 5: (high, 2)}
 
     def phase_two(p, _):
         for x, cut in gets.items():
@@ -280,7 +292,7 @@
         for x in range(CUTS):
             @pl.when(p == x * PER_CUT)
             def _():
-                if length > 1:
+                if length > 1 and x < CUTS - 1:
                     arrive(0, length - 1, x)
 
         near(p, pk, pv, False)
@@ -291,11 +303,15 @@
                 if x in passes:
                     for d in passes[x][0]:
                         relay(1, d, passes[x][1])
-                if x in gets:
+                if x in gets and gets[x] < CUTS - 1:
                     send(1, gets[x])
         return 0
 
-    lax.fori_loop(0, PAIRS, phase_two, 0)
+    split = PAIRS - PER_CUT
+    lax.fori_loop(0, split, phase_two, 0)
+    if length > 1:
+        arrive(0, length - 1, CUTS - 1)
+        cross(length - 1, lambda c: c.start())
     if n > group:
         for i in range(n - group):
             far_copy(i, True).wait_recv()
@@ -304,8 +320,8 @@
         for x in range(CUTS):
             @pl.when(p == x * PER_CUT)
             def _():
-                if length > 1:
-                    arrive(1, length - 1, x)
+                for d in range(1 if x == CUTS - 1 else max(1, length - 1), length):
+                    arrive(1, d, x)
 
         middle(p, 1)
         far(p)
@@ -314,20 +330,20 @@
             span = slice(t * TILE, (t + 1) * TILE)
             res = (num[span, cols] / den[span, cols]).astype(jnp.bfloat16)
             out_ref[span, cols] = jnp.dot(back[...], res, preferred_element_type=jnp.float32).astype(jnp.bfloat16)
-
-        @pl.when(p == 1)
-        def _():
-            for d in high:
-                relay(1, d, CUTS - 1)
         return 0
 
-    lax.fori_loop(0, PAIRS, phase_three, 0)
+    early_split = split - PER_CUT
+    lax.fori_loop(0, early_split, phase_three, 0)
+    lax.fori_loop(split, PAIRS, phase_two, 0)
+    lax.fori_loop(early_split, PAIRS, phase_three, 0)
     for cut in range(CUTS):
         for which in range(2):
             near_copy(cut, which).wait_send()
-        for u in range(2):
+        for u in range(2 if cut < CUTS - 1 else 1):
             for d in range(max(1, length - 1)):
                 both(u, d, cut, lambda c: c.wait_send())
+    for d in range(1, length):
+        cross(d, lambda c: c.wait_send())
     for i in range(n - group):
         far_copy(i).wait_send()
 
@@ -365,6 +381,7 @@
             dma((group, CUTS)),
             dma((spare + 1,)),
             dma((spare + 1,)),
+            dma((2, length)),
         ],
         compiler_params=pltpu.CompilerParams(collective_id=0, has_side_effects=True, vmem_limit_bytes=62 << 20),
     )(queries, keys, values)

time: 161 us -> 154 us (0.957)
  Pallas kernels: 156 us -> 150 us
    pallas_call x1, Pallas kernels: 156 us -> 150 us  [per_device(): pl.pallas_call(functools.partial(kernel, n, group), out_shape=(jax.ShapeD...]
where the time goes in v3:
time: 154 us
  Pallas kernels  150 us (97%)
  local copies, waits for them, and re-layouts  3.75 us (2%)
    pallas_call x1, Pallas kernels, per_device(): pl.pallas_call(functools.partial(kernel, n, group), out_shape=(jax.ShapeD...  150 us
    unnamed x4, local copies, waits for them, and re-layouts  3.75 us

profile of v3, /device:TPU:0, one launch (start us, length us, event | category | flops | bytes accessed | tf_op | source)
XLA Modules:
  0.0 154.1 jit_solution(3086158473231892256)
XLA Ops:
  0.6 149.7 %shard_map.50 = (bf16[1024,1024]{1,0:T(8,128)(2,1)}, bf16[32,1024]{1,0:T(8,128)(2,1)}) custom-call(bf16[1024,1024]{1,0:T(8,128)(2,1)} %q_ref.1, bf16[1024,1024]{1,0:T(8,128)(2,1)} %k_ref.1, bf16[1024,1024]{1,0:T(8,128)(2,1)} %v_ref.1), custom_call_target="tpu_custom_call" | custom-call | tf_op jit(solution)/shard_map/pallas_call | solution.py:359
  150.4 0.0 copy-start
  150.4 3.1 %copy.7 = bf16[1024,1024]{1,0:T(8,128)(2,1)} copy(bf16[1024,1024]{1,0:T(8,128)(2,1)} %get-tuple-element.4) | data formatting | bytes 4194304
  153.5 0.0 copy-done
  153.5 0.6 copy.8
Async XLA Ops:
  150.4 3.1 %copy-start = (bf16[32,1024]{1,0:T(8,128)(2,1)S(1)}, bf16[32,1024]{1,0:T(8,128)(2,1)}, u32[]{:S(2)}) copy-start(bf16[32,1024]{1,0:T(8,128)(2,1)} %get-tuple-element.5) | copy-start | bytes 196612
